TPU v7x, 512 devices: a whole 4x8x8 slice. The times are simulated.
512 devices in a mesh: dp: 4 (over x), row: 32 (over y, z_hi, core), col: 4 (over z_lo).
Axes of the slice: x: 4, y: 8, z: 8 (z_hi: 2, z_lo: 4; z = z_hi * 4 + z_lo), core: 2. Of those that a mesh axis runs over, the one named last changes fastest.
Arguments:
- tokens: bfloat16 [2048, 8192], P('dp', ('row', 'col')), may hold values from -6 to 6
- hidden_grad: bfloat16 [2048, 6656], P(('dp', 'row'), 'col'), may hold values from -6 to 6
- gate_weight: bfloat16 [8192, 6656], P('row', 'col'), may hold values from -0.0625 to 0.0625
- up_weight: bfloat16 [8192, 6656], P('row', 'col'), may hold values from -0.0625 to 0.0625
Outputs:
- input_grad: bfloat16 [2048, 8192], P('dp', ('row', 'col'))
- gate_grad: bfloat16 [8192, 6656], P('row', 'col')
- up_grad: bfloat16 [8192, 6656], P('row', 'col')
All inputs are finite; a program needn't handle non-finite values.
Results may differ from a plain program's by a relative error of at most 0.022.
Values may be sent and summed in bfloat16 or wider, within the bound.
A program may use at most 64 MiB of HBM per device.

v0:
```python
import jax
import jax.numpy as jnp
from jax import lax
from jax.sharding import PartitionSpec as P


def contract_rows(left, right):
    return lax.dot_general(
        left, right, (((0,), (0,)), ((), ())), preferred_element_type=jnp.float32
    )


def contract_cols(left, right):
    return lax.dot_general(
        left, right, (((1,), (1,)), ((), ())), preferred_element_type=jnp.float32
    )


def body(tokens, hidden_grad, gate_weight, up_weight):
    panel = lax.all_gather(tokens, "col", axis=1, tiled=True)
    width = gate_weight.shape[1]
    shares = lax.psum_scatter(
        jnp.concatenate(
            [
                jnp.dot(panel, gate_weight, preferred_element_type=jnp.float32),
                jnp.dot(panel, up_weight, preferred_element_type=jnp.float32),
            ],
            axis=1,
        ).astype(jnp.bfloat16),
        "row",
        scatter_dimension=0,
        tiled=True,
    ).astype(jnp.float32)
    gate = shares[:, :width]
    up = shares[:, width:]
    sigma = jax.nn.sigmoid(gate)
    upstream = hidden_grad.astype(jnp.float32)
    gate_act = (upstream * up * sigma * (1.0 + gate * (1.0 - sigma))).astype(jnp.bfloat16)
    up_act = (upstream * gate * sigma).astype(jnp.bfloat16)
    gate_panel, up_panel = (
        lax.all_gather(gate_act, "row", axis=0, tiled=True),
        lax.all_gather(up_act, "row", axis=0, tiled=True),
    )
    input_share = lax.psum_scatter(
        (contract_cols(gate_weight, gate_panel) + contract_cols(up_weight, up_panel)).astype(
            jnp.bfloat16
        ),
        "col",
        scatter_dimension=0,
        tiled=True,
    ).astype(jnp.float32)
    input_grad = input_share.T.astype(jnp.bfloat16)
    gate_local = contract_rows(panel, gate_panel)
    up_local = contract_rows(panel, up_panel)
    gate_sum, up_sum = (
        lax.psum(gate_local.astype(jnp.bfloat16), "dp").astype(jnp.float32),
        lax.psum(up_local.astype(jnp.bfloat16), "dp").astype(jnp.float32),
    )
    return (input_grad, gate_sum.astype(jnp.bfloat16), up_sum.astype(jnp.bfloat16))


def solution(mesh):
    return jax.shard_map(
        body,
        mesh=mesh,
        in_specs=(
            P("dp", ("row", "col")),
            P(("dp", "row"), "col"),
            P("row", "col"),
            P("row", "col"),
        ),
        out_specs=(P("dp", ("row", "col")), P("row", "col"), P("row", "col")),
        check_vma=False,
    )
```

profile of v0, /device:TPU:2, one launch (start us, length us, event | category | flops | bytes accessed | tf_op | source)
XLA Modules:
  0.0 454.6 jit_solution(16732908509172800166)
XLA Ops:
  7.2 0.0 copy-start
  7.2 0.0 reduce-scatter.5.cloned.1.call-start
  7.2 16.8 %all_gather.9 = bf16[512,256]{0,1:T(8,128)(2,1)S(1)} all-gather(bf16[512,64]{0,1:T(8,128)(2,1)} %param.4), channel_id=1, replica_groups=mesh['dp'=4,'row'=32,'col'=4] {'col'}, dimensions={1}, use_global_device_ids=true | all-gather | bytes 327680 | tf_op jit(solution)/shard_map/all_gather | solution.py:20
  24.0 1.8 convolution_convert_fusion
  25.8 0.0 copy-done
  25.9 0.7 convolution_convert_fusion.1
  26.5 1.9 pad_maximum_fusion
  28.5 0.0 reduce-scatter.5.cloned.1.call-update
  28.5 0.0 all-gather.3.cloned.1.call-start
  28.6 149.2 %reduce-scatter.5.cloned.1.call-done = bf16[16,3328]{1,0:T(8,128)(2,1)} async-done(((bf16[512,3328]{1,0:T(8,128)(2,1)}), bf16[16,3328]{1,0:T(8,128)(2,1)}) %reduce-scatter.5.cloned.1.call-update) | async-done | bytes 106512 | tf_op jit(solution)/shard_map/reduce_scatter | solution.py:22
  177.7 0.9 convert_element_type.41
  178.6 0.0 copy-done.4
  178.6 0.7 fusion.8
  179.3 0.0 all-gather.3.cloned.1.call-update
  179.4 0.0 all-gather.5.cloned.1.call-start
  179.4 0.7 all-gather.5.cloned.1.call-update
  180.1 0.0 all-reduce.3.cloned.1.call-start
  180.1 87.8 %all-gather.3.cloned.1.call-done = bf16[512,1664]{1,0:T(8,128)(2,1)} async-done(((bf16[16,1664]{1,0:T(8,128)(2,1)}), bf16[512,1664]{1,0:T(8,128)(2,1)}) %all-gather.3.cloned.1.call-update) | async-done | bytes 1703952 | tf_op jit(solution)/shard_map/all_gather | solution.py:41
  267.9 3.0 fusion
  271.0 86.0 %all-gather.5.cloned.1.call-done = bf16[512,1664]{1,0:T(8,128)(2,1)} async-done(((bf16[16,1664]{1,0:T(8,128)(2,1)}), bf16[512,1664]{1,0:T(8,128)(2,1)}) %all-gather.5.cloned.1.call-update) | async-done | bytes 1703952 | tf_op jit(solution)/shard_map/all_gather | solution.py:42
  357.0 3.0 fusion.1
  360.0 0.0 all-reduce.3.cloned.1.call-update
  360.0 0.0 copy-start.2
  360.0 0.0 reduce-scatter.7.cloned.1.call-start
  360.1 2.3 fusion.9
  362.4 1.4 fusion.3
  363.8 1.8 copy.13
  365.6 0.0 reduce-scatter.7.cloned.1.call-update
  365.6 49.9 %all-reduce.3.cloned.1.call-done = (bf16[256,1664]{0,1:T(8,128)(2,1)}, bf16[256,1664]{0,1:T(8,128)(2,1)}) async-done(((bf16[256,1664]{0,1:T(8,128)(2,1)}, bf16[256,1664]{0,1:T(8,128)(2,1)}), (bf16[256,1664]{0,1:T(8,128)(2,1)}, bf16[256,1664]{0,1:T(8,128)(2,1)})) %all-reduce.3.cloned.1.call-update) | async-done | bytes 1703952 | tf_op jit(solution)/shard_map/psum | solution.py:56
  415.5 2.3 copy.11
  417.8 1.3 copy.12
  419.1 28.9 %reduce-scatter.7.cloned.1.call-done = bf16[64,512]{1,0:T(8,128)(2,1)} async-done(((bf16[256,512]{1,0:T(8,128)(2,1)}), bf16[64,512]{1,0:T(8,128)(2,1)}) %reduce-scatter.7.cloned.1.call-update) | async-done | bytes 65552
  (6 shorter events, 0.0 us)
Async XLA Ops:
  7.2 18.7 %copy-start = (bf16[256,1664]{1,0:T(8,128)(2,1)S(1)}, bf16[256,1664]{1,0:T(8,128)(2,1)}, u32[]{:S(2)}) copy-start(bf16[256,1664]{1,0:T(8,128)(2,1)} %param.6) | copy-start | bytes 2555908
  7.2 170.5 %reduce-scatter.5.cloned.1.call-start = ((), (), s32[]{:S(2)}) async-start(), calls=%async_computation.2 | async-start | bytes 3514368 | tf_op jit(solution)/shard_map/reduce_scatter | solution.py:22
  28.5 150.2 %copy-start.4 = (bf16[16,1664]{1,0:T(8,128)(2,1)S(1)}, bf16[16,1664]{1,0:T(8,128)(2,1)}, u32[]{:S(2)}) copy-start(bf16[16,1664]{1,0:T(8,128)(2,1)} %param.5) | copy-start | bytes 159748
  28.5 239.4 %all-gather.3.cloned.1.call-start = ((), (), s32[]{:S(2)}) async-start(), calls=%async_computation.3 | async-start | bytes 1757184 | tf_op jit(solution)/shard_map/all_gather | solution.py:41
  179.4 177.6 %all-gather.5.cloned.1.call-start = ((), (), s32[]{:S(2)}) async-start(), calls=%async_computation.4 | async-start | bytes 1757184 | tf_op jit(solution)/shard_map/all_gather | solution.py:42
  180.1 235.4 %all-reduce.3.cloned.1.call-start = ((), (), s32[]{:S(2)}) async-start(), calls=%async_computation.6 | async-start | bytes 3407872 | tf_op jit(solution)/shard_map/psum | solution.py:56
  360.0 2.4 copy-start.1
  360.0 2.4 copy-start.2
  360.0 88.0 %reduce-scatter.7.cloned.1.call-start = ((), (), s32[]{:S(2)}) async-start(), calls=%async_computation.5 | async-start | bytes 327680
  415.5 2.3 copy-start.3
Sparse Core Ops, SparseCore 0:
  28.6 149.0 reduce-scatter.4
  181.6 86.3 all-gather.2
  271.8 85.1 all-gather.4
  360.1 55.3 all-reduce.2
  418.7 29.2 reduce-scatter.6
where the time goes:
time: 455 us
  waiting for transfers between devices  403 us (89%)
  blocking collectives  16.8 us (4%)
  between operations  13.9 us (3%)
  matrix products  12.2 us (3%)
  local copies, waits for them, and re-layouts  5.43 us (1%)
    reduce_scatter x1, waiting for transfers between devices, body(): lax.psum_scatter(jnp.concatenate([jnp.dot(panel, gate_weight, preferred_e...  149 us
    all_gather x1, waiting for transfers between devices, body(): lax.all_gather(gate_act, 'row', axis=0, tiled=True)  87.8 us
    all_gather x1, waiting for transfers between devices, body(): lax.all_gather(up_act, 'row', axis=0, tiled=True)  86 us
    psum x1, waiting for transfers between devices, body(): lax.psum(gate_local.astype(jnp.bfloat16), 'dp').astype(jnp.float32)  49.9 us
    unnamed x6, waiting for transfers between devices  29.7 us
    all_gather x1, blocking collectives, body(): panel = lax.all_gather(tokens, 'col', axis=1, tiled=True)  16.8 us
  transfers between devices with their start and end apart: 5, of which 5 were waited for; matrix products, arithmetic and copies ran while one was open for 3% of the time, Pallas kernels for 0%

commit v1 on v0

--- a/solution.py
+++ b/solution.py
@@ -38,7 +38,9 @@
     gate_act = (upstream * up * sigma * (1.0 + gate * (1.0 - sigma))).astype(jnp.bfloat16)
     up_act = (upstream * gate * sigma).astype(jnp.bfloat16)
     gate_panel, up_panel = (
-        lax.all_gather(gate_act, "row", axis=0, tiled=True),
+        jnp.concatenate(
+            lax.all_to_all(jnp.stack([gate_act] * lax.axis_size("row")), "row", 0, 0), axis=0
+        ),
         lax.all_gather(up_act, "row", axis=0, tiled=True),
     )
     input_share = lax.psum_scatter(

time: 455 us -> 396 us (0.87)
  waiting for transfers between devices: 403 us -> 338 us
  starting transfers between devices: 0.2 us -> 6.17 us
    all_gather x1 -> x0, waiting for transfers between devices: 87.8 us -> none  [body(): lax.all_gather(gate_act, 'row', axis=0, tiled=True)]
    all_to_all x0 -> x1, waiting for transfers between devices: none -> 46.8 us  [body(): lax.all_to_all(jnp.stack([gate_act] * lax.axis_size('row')), 'row', 0, 0)]
    all_gather x1, waiting for transfers between devices: 86 us -> 62.1 us  [body(): lax.all_gather(up_act, 'row', axis=0, tiled=True)]
    all_to_all x0 -> x1, starting transfers between devices: none -> 6.01 us  [body(): lax.all_to_all(jnp.stack([gate_act] * lax.axis_size('row')), 'row', 0, 0)]
    unnamed x6 -> x5, waiting for transfers between devices: 29.7 us -> 29.7 us
where the time goes in v1:
time: 396 us; the launch traced here: 395 us
  waiting for transfers between devices  338 us (85%)
  blocking collectives  16.8 us (4%)
  between operations  13.9 us (4%)
  matrix products  10.7 us (3%)
  local copies, waits for them, and re-layouts  6.73 us (2%)
  starting transfers between devices  6.17 us (2%)
    reduce_scatter x1, waiting for transfers between devices, body(): lax.psum_scatter(jnp.concatenate([jnp.dot(panel, gate_weight, preferred_e...  149 us
    all_gather x1, waiting for transfers between devices, body(): lax.all_gather(up_act, 'row', axis=0, tiled=True)  62.1 us
    psum x1, waiting for transfers between devices, body(): lax.psum(gate_local.astype(jnp.bfloat16), 'dp').astype(jnp.float32)  49.9 us
    all_to_all x1, waiting for transfers between devices, body(): lax.all_to_all(jnp.stack([gate_act] * lax.axis_size('row')), 'row', 0, 0)  46.8 us
    unnamed x5, waiting for transfers between devices  29.7 us
    all_gather x1, blocking collectives, body(): panel = lax.all_gather(tokens, 'col', axis=1, tiled=True)  16.8 us
  transfers between devices with their start and end apart: 5, of which 5 were waited for; matrix products, arithmetic and copies ran while one was open for 3% of the time, Pallas kernels for 0%

profile of v1, /device:TPU:2, one launch (start us, length us, event | category | flops | bytes accessed | tf_op | source)
XLA Modules:
  0.0 395.5 jit_solution(11719735316217172535)
XLA Ops:
  7.2 0.0 copy-start
  7.2 0.0 reduce-scatter.5.cloned.1.call-start
  7.2 16.8 %all_gather.6 = bf16[512,256]{0,1:T(8,128)(2,1)S(1)} all-gather(bf16[512,64]{0,1:T(8,128)(2,1)} %param.4), channel_id=1, replica_groups=mesh['dp'=4,'row'=32,'col'=4] {'col'}, dimensions={1}, use_global_device_ids=true | all-gather | bytes 327680 | tf_op jit(solution)/shard_map/all_gather | solution.py:20
  24.0 1.8 convolution_convert_fusion
  25.9 0.0 copy-done
  25.9 0.7 convolution_convert_fusion.1
  26.5 1.9 pad_maximum_fusion
  28.5 0.0 reduce-scatter.5.cloned.1.call-update
  28.5 149.2 %reduce-scatter.5.cloned.1.call-done = bf16[16,3328]{1,0:T(8,128)(2,1)} async-done(((bf16[512,3328]{1,0:T(8,128)(2,1)}), bf16[16,3328]{1,0:T(8,128)(2,1)}) %reduce-scatter.5.cloned.1.call-update) | async-done | bytes 106512 | tf_op jit(solution)/shard_map/reduce_scatter | solution.py:22
  177.7 0.9 convert_element_type.41
  178.6 0.7 fusion.8
  179.3 1.3 stack.2
  180.6 6.0 %all-to-all-start = ((bf16[32,16,1664]{2,1,0:T(8,128)(2,1)}), bf16[32,16,1664]{2,1,0:T(8,128)(2,1)S(1)}, u32[]{:S(2)}, u32[]{:S(2)}) async-start(bf16[32,16,1664]{2,1,0:T(8,128)(2,1)} %stack.2), calls=%async_computation.1 | async-start | bytes 3407872 | tf_op jit(solution)/shard_map/all_to_all | solution.py:42
  186.6 0.0 all-gather.2.cloned.1.call-start
  186.7 0.7 all-gather.2.cloned.1.call-update
  187.4 0.0 all-reduce.3.cloned.1.call-start
  187.4 46.8 %all-to-all-done = bf16[32,16,1664]{2,1,0:T(8,128)(2,1)S(1)} async-done(((bf16[32,16,1664]{2,1,0:T(8,128)(2,1)}), bf16[32,16,1664]{2,1,0:T(8,128)(2,1)S(1)}, u32[]{:S(2)}, u32[]{:S(2)}) %all-to-all-start) | async-done | bytes 1703968 | tf_op jit(solution)/shard_map/all_to_all | solution.py:42
  234.2 1.6 fusion
  235.8 62.1 %all-gather.2.cloned.1.call-done = bf16[512,1664]{1,0:T(8,128)(2,1)} async-done(((bf16[16,1664]{1,0:T(8,128)(2,1)}), bf16[512,1664]{1,0:T(8,128)(2,1)}) %all-gather.2.cloned.1.call-update) | async-done | bytes 1703952 | tf_op jit(solution)/shard_map/all_gather | solution.py:44
  297.9 3.0 fusion.1
  300.9 0.0 copy-done.2
  300.9 0.0 all-reduce.3.cloned.1.call-update
  300.9 0.0 copy-start.3
  300.9 0.0 reduce-scatter.7.cloned.1.call-start
  301.0 2.3 fusion.9
  303.3 1.4 fusion.3
  304.7 1.8 copy.13
  306.5 0.0 reduce-scatter.7.cloned.1.call-update
  306.5 49.9 %all-reduce.3.cloned.1.call-done = (bf16[256,1664]{0,1:T(8,128)(2,1)}, bf16[256,1664]{0,1:T(8,128)(2,1)}) async-done(((bf16[256,1664]{0,1:T(8,128)(2,1)}, bf16[256,1664]{0,1:T(8,128)(2,1)}), (bf16[256,1664]{0,1:T(8,128)(2,1)}, bf16[256,1664]{0,1:T(8,128)(2,1)})) %all-reduce.3.cloned.1.call-update) | async-done | bytes 1703952 | tf_op jit(solution)/shard_map/psum | solution.py:58
  356.4 2.3 copy.11
  358.7 1.3 copy.12
  360.0 28.9 %reduce-scatter.7.cloned.1.call-done = bf16[64,512]{1,0:T(8,128)(2,1)} async-done(((bf16[256,512]{1,0:T(8,128)(2,1)}), bf16[64,512]{1,0:T(8,128)(2,1)}) %reduce-scatter.7.cloned.1.call-update) | async-done | bytes 65552
  (8 shorter events, 0.0 us)
Async XLA Ops:
  7.2 18.7 %copy-start = (bf16[256,1664]{1,0:T(8,128)(2,1)S(1)}, bf16[256,1664]{1,0:T(8,128)(2,1)}, u32[]{:S(2)}) copy-start(bf16[256,1664]{1,0:T(8,128)(2,1)} %param.6) | copy-start | bytes 2555908
  7.2 170.5 %reduce-scatter.5.cloned.1.call-start = ((), (), s32[]{:S(2)}) async-start(), calls=%async_computation.3 | async-start | bytes 3514368 | tf_op jit(solution)/shard_map/reduce_scatter | solution.py:22
  28.5 150.2 %copy-start.5 = (bf16[16,1664]{1,0:T(8,128)(2,1)S(1)}, bf16[16,1664]{1,0:T(8,128)(2,1)}, u32[]{:S(2)}) copy-start(bf16[16,1664]{1,0:T(8,128)(2,1)} %param.5) | copy-start | bytes 159748
  180.6 53.6 %all-to-all-start = ((bf16[32,16,1664]{2,1,0:T(8,128)(2,1)}), bf16[32,16,1664]{2,1,0:T(8,128)(2,1)S(1)}, u32[]{:S(2)}, u32[]{:S(2)}) async-start(bf16[32,16,1664]{2,1,0:T(8,128)(2,1)} %stack.2), calls=%async_computation.1 | async-start | bytes 3407872 | tf_op jit(solution)/shard_map/all_to_all | solution.py:42
  186.6 111.2 %all-gather.2.cloned.1.call-start = ((), (), s32[]{:S(2)}) async-start(), calls=%async_computation.4 | async-start | bytes 1757184 | tf_op jit(solution)/shard_map/all_gather | solution.py:44
  187.4 169.0 %all-reduce.3.cloned.1.call-start = ((), (), s32[]{:S(2)}) async-start(), calls=%async_computation.6 | async-start | bytes 3407872 | tf_op jit(solution)/shard_map/psum | solution.py:58
  234.2 66.7 %copy-start.2 = (bf16[32,16,1664]{2,1,0:T(8,128)(2,1)}, bf16[32,16,1664]{2,1,0:T(8,128)(2,1)S(1)}, u32[]{:S(2)}) copy-start(bf16[32,16,1664]{2,1,0:T(8,128)(2,1)S(1)} %all-to-all-done) | copy-start | bytes 5111812
  300.9 2.4 copy-start.1
  300.9 2.4 copy-start.3
  300.9 88.0 %reduce-scatter.7.cloned.1.call-start = ((), (), s32[]{:S(2)}) async-start(), calls=%async_computation.5 | async-start | bytes 327680
  356.4 2.3 copy-start.4
Sparse Core Ops, SparseCore 0:
  28.6 149.0 reduce-scatter.4
  191.3 106.5 all-gather.1
  301.0 55.3 all-reduce.2
  359.6 29.2 reduce-scatter.6

commit v2 on v0

--- a/solution.py
+++ b/solution.py
@@ -53,7 +53,7 @@
     gate_local = contract_rows(panel, gate_panel)
     up_local = contract_rows(panel, up_panel)
     gate_sum, up_sum = (
-        lax.psum(gate_local.astype(jnp.bfloat16), "dp").astype(jnp.float32),
+        jnp.sum(lax.all_gather(gate_local.astype(jnp.bfloat16), "dp"), axis=0).astype(jnp.float32),
         lax.psum(up_local.astype(jnp.bfloat16), "dp").astype(jnp.float32),
     )
     return (input_grad, gate_sum.astype(jnp.bfloat16), up_sum.astype(jnp.bfloat16))

time: 455 us -> 502 us (1.10)
  waiting for transfers between devices: 403 us -> 434 us
  other arithmetic: 3.55 us -> 12.9 us
  local copies, waits for them, and re-layouts: 5.43 us -> 11.9 us
    all_gather x0 -> x1, waiting for transfers between devices: none -> 51.5 us  [body(): lax.all_gather(gate_local.astype(jnp.bfloat16), 'dp')]
    unnamed x6 -> x7, waiting for transfers between devices: 29.7 us -> 15.8 us
    reduce_sum x0 -> x1, other arithmetic: none -> 9.35 us  [body(): jnp.sum(lax.all_gather(gate_local.astype(jnp.bfloat16), 'dp'), axis=0)]
    all_gather x0 -> x1, local copies, waits for them, and re-layouts: none -> 7.43 us  [body(): lax.all_gather(gate_local.astype(jnp.bfloat16), 'dp')]
    psum x1, waiting for transfers between devices: 49.9 us -> 44 us  [body(): lax.psum(up_local.astype(jnp.bfloat16), 'dp').astype(jnp.float32)]
  transfers between devices with their start and end apart: 5 -> 6, of which waited for: 5 -> 6; matrix products, arithmetic and copies ran while one was open for 3% -> 6% of each run, Pallas kernels for 0% -> 0%
where the time goes in v2:
time: 502 us
  waiting for transfers between devices  434 us (86%)
  blocking collectives  16.8 us (3%)
  between operations  14.2 us (3%)
  other arithmetic  12.9 us (3%)
  local copies, waits for them, and re-layouts  11.9 us (2%)
  matrix products  11.5 us (2%)
    reduce_scatter x1, waiting for transfers between devices, body(): lax.psum_scatter(jnp.concatenate([jnp.dot(panel, gate_weight, preferred_e...  149 us
    all_gather x1, waiting for transfers between devices, body(): lax.all_gather(up_act, 'row', axis=0, tiled=True)  87.8 us
    all_gather x1, waiting for transfers between devices, body(): lax.all_gather(gate_act, 'row', axis=0, tiled=True)  85.9 us
    all_gather x1, waiting for transfers between devices, body(): lax.all_gather(gate_local.astype(jnp.bfloat16), 'dp')  51.5 us
    psum x1, waiting for transfers between devices, body(): lax.psum(up_local.astype(jnp.bfloat16), 'dp').astype(jnp.float32)  44 us
    all_gather x1, blocking collectives, body(): panel = lax.all_gather(tokens, 'col', axis=1, tiled=True)  16.8 us
    unnamed x7, waiting for transfers between devices  15.8 us
  transfers between devices with their start and end apart: 6, of which 6 were waited for; matrix products, arithmetic and copies ran while one was open for 6% of the time, Pallas kernels for 0%

profile of v2, /device:TPU:2, one launch (start us, length us, event | category | flops | bytes accessed | tf_op | source)
XLA Modules:
  0.0 501.7 jit_solution(2145514143370672330)
XLA Ops:
  7.2 0.0 reduce-scatter.5.cloned.1.call-start
  7.2 16.8 %all_gather.15 = bf16[512,256]{0,1:T(8,128)(2,1)S(1)} all-gather(bf16[512,64]{0,1:T(8,128)(2,1)} %param.4), channel_id=1, replica_groups=mesh['dp'=4,'row'=32,'col'=4] {'col'}, dimensions={1}, use_global_device_ids=true | all-gather | bytes 327680 | tf_op jit(solution)/shard_map/all_gather | solution.py:20
  24.0 1.8 convolution_convert_fusion
  25.9 0.7 convolution_convert_fusion.1
  26.5 1.9 pad_maximum_fusion
  28.5 0.0 reduce-scatter.5.cloned.1.call-update
  28.5 0.0 all-gather.7.cloned.1.call-start
  28.6 149.2 %reduce-scatter.5.cloned.1.call-done = bf16[16,3328]{1,0:T(8,128)(2,1)} async-done(((bf16[512,3328]{1,0:T(8,128)(2,1)}), bf16[16,3328]{1,0:T(8,128)(2,1)}) %reduce-scatter.5.cloned.1.call-update) | async-done | bytes 106512 | tf_op jit(solution)/shard_map/reduce_scatter | solution.py:22
  177.7 0.9 convert_element_type.43
  178.6 0.7 fusion.8
  179.3 0.0 all-gather.7.cloned.1.call-update
  179.4 0.0 all-gather.5.cloned.1.call-start
  179.4 0.7 all-gather.5.cloned.1.call-update
  180.1 0.0 all-reduce.2.cloned.1.call-start
  180.2 87.8 %all-gather.7.cloned.1.call-done = bf16[512,1664]{1,0:T(8,128)(2,1)} async-done(((bf16[16,1664]{1,0:T(8,128)(2,1)}), bf16[512,1664]{1,0:T(8,128)(2,1)}) %all-gather.7.cloned.1.call-update) | async-done | bytes 1703952 | tf_op jit(solution)/shard_map/all_gather | solution.py:42
  268.0 3.0 fusion.1
  271.0 0.0 all-reduce.2.cloned.1.call-update
  271.0 0.0 all-gather.9.cloned.1.call-start
  271.0 85.9 %all-gather.5.cloned.1.call-done = bf16[512,1664]{1,0:T(8,128)(2,1)} async-done(((bf16[16,1664]{1,0:T(8,128)(2,1)}), bf16[512,1664]{1,0:T(8,128)(2,1)}) %all-gather.5.cloned.1.call-update) | async-done | bytes 1703952 | tf_op jit(solution)/shard_map/all_gather | solution.py:41
  357.0 3.0 fusion
  360.0 0.0 reduce-scatter.7.cloned.1.call-start
  360.1 2.3 fusion.9
  362.4 0.7 fusion.3
  363.1 0.9 copy.12
  364.0 0.0 reduce-scatter.7.cloned.1.call-update
  364.0 44.0 %all-reduce.2.cloned.1.call-done = bf16[256,1664]{0,1:T(8,128)(2,1)} async-done(((bf16[256,1664]{0,1:T(8,128)(2,1)}), bf16[256,1664]{0,1:T(8,128)(2,1)}) %all-reduce.2.cloned.1.call-update) | async-done | bytes 851984 | tf_op jit(solution)/shard_map/psum | solution.py:57
  408.0 2.2 copy.11
  410.2 51.5 %all-gather.9.cloned.1.call-done = bf16[1024,1664]{0,1:T(8,128)(2,1)} async-done(((bf16[256,1664]{0,1:T(8,128)(2,1)}), bf16[1024,1664]{0,1:T(8,128)(2,1)}) %all-gather.9.cloned.1.call-update) | async-done | bytes 3407888 | tf_op jit(solution)/shard_map/all_gather | solution.py:56
  461.7 7.4 %reshape.6 = bf16[4,256,1664]{1,0,2:T(4,128)(2,1)} reshape(bf16[1024,1664]{0,1:T(8,128)(2,1)} %all-gather.9.cloned.1.call-done) | data formatting | bytes 6815744 | tf_op jit(solution)/shard_map/all_gather | solution.py:56
  469.1 9.3 %reduce_sum.12 = bf16[256,1664]{0,1:T(8,128)(2,1)S(1)} reduce(bf16[4,256,1664]{1,0,2:T(4,128)(2,1)} %reshape.6, bf16[]{:T(256)} %constant.4.clone.1), dimensions={0}, to_apply=%region_2.0 | reduce | flops 1277952 | bytes 4259842 | tf_op jit(solution)/shard_map/reduce_sum | solution.py:56
  478.5 1.4 copy.10
  479.8 15.0 %reduce-scatter.7.cloned.1.call-done = bf16[64,512]{1,0:T(8,128)(2,1)} async-done(((bf16[256,512]{1,0:T(8,128)(2,1)}), bf16[64,512]{1,0:T(8,128)(2,1)}) %reduce-scatter.7.cloned.1.call-update) | async-done | bytes 65552
  (9 shorter events, 0.0 us)
Async XLA Ops:
  7.2 18.7 %copy-start = (bf16[256,1664]{1,0:T(8,128)(2,1)S(1)}, bf16[256,1664]{1,0:T(8,128)(2,1)}, u32[]{:S(2)}) copy-start(bf16[256,1664]{1,0:T(8,128)(2,1)} %param.6) | copy-start | bytes 2555908
  7.2 170.5 %reduce-scatter.5.cloned.1.call-start = ((), (), s32[]{:S(2)}) async-start(), calls=%async_computation.2 | async-start | bytes 3514368 | tf_op jit(solution)/shard_map/reduce_scatter | solution.py:22
  28.5 150.2 %copy-start.3 = (bf16[16,1664]{1,0:T(8,128)(2,1)S(1)}, bf16[16,1664]{1,0:T(8,128)(2,1)}, u32[]{:S(2)}) copy-start(bf16[16,1664]{1,0:T(8,128)(2,1)} %param.5) | copy-start | bytes 159748
  28.5 239.4 %all-gather.7.cloned.1.call-start = ((), (), s32[]{:S(2)}) async-start(), calls=%async_computation.4 | async-start | bytes 1757184 | tf_op jit(solution)/shard_map/all_gather | solution.py:42
  179.4 177.6 %all-gather.5.cloned.1.call-start = ((), (), s32[]{:S(2)}) async-start(), calls=%async_computation.3 | async-start | bytes 1757184 | tf_op jit(solution)/shard_map/all_gather | solution.py:41
  180.1 227.9 %all-reduce.2.cloned.1.call-start = ((), (), s32[]{:S(2)}) async-start(), calls=%async_computation.5 | async-start | bytes 1703936 | tf_op jit(solution)/shard_map/psum | solution.py:57
  271.0 190.7 %all-gather.9.cloned.1.call-start = ((), (), s32[]{:S(2)}) async-start(), calls=%async_computation.6 | async-start | bytes 4259840 | tf_op jit(solution)/shard_map/all_gather | solution.py:56
  360.0 2.4 copy-start.1
  360.0 134.8 %reduce-scatter.7.cloned.1.call-start = ((), (), s32[]{:S(2)}) async-start(), calls=%async_computation.7 | async-start | bytes 327680
  360.1 2.3 copy-start.2
Sparse Core Ops, SparseCore 0:
  28.6 149.0 reduce-scatter.4
  181.6 86.3 all-gather.6
  271.8 85.1 all-gather.4
  359.8 48.1 all-reduce.1
  410.5 51.1 all-gather.8
  464.9 29.8 reduce-scatter.6
